TPU v7x, 512 devices: a whole 4x4x16 slice. The times are simulated.
512 devices in a mesh: section: 8 (over z_lo), dp: 16 (over x, z_hi, core), tensor: 4 (over y).
Axes of the slice: x: 4, y: 4, z: 16 (z_hi: 2, z_lo: 8; z = z_hi * 8 + z_lo), core: 2. Of those that a mesh axis runs over, the one named last changes fastest.
Arguments:
- norm_in: bfloat16 [8, 2048, 8192], P('section', 'dp', 'tensor'), may hold values from -20 to 20
- query_grad: bfloat16 [8, 2048, 4096], P('section', 'dp', 'tensor'), may hold values from -20 to 20
- attn_out: bfloat16 [8, 2048, 4096], P('section', 'dp', 'tensor'), may hold values from -20 to 20
- handed: bfloat16 [8, 2048, 8192], P('section', 'dp', 'tensor'), may hold values from -20 to 20
- sketch_q: bfloat16 [8, 64, 4096], P('section', None, 'tensor'), may hold values from -6 to 6
- sketch_o: bfloat16 [8, 64, 8192], P('section', None, 'tensor'), may hold values from -6 to 6
Outputs:
- lora_b_q: bfloat16 [8, 64, 8192], P('section', None, 'tensor')
- lora_a_q: float32 [8, 64, 4096], P('section', None, 'tensor')
- lora_b_o: bfloat16 [8, 64, 4096], P('section', None, 'tensor')
- lora_a_o: float32 [8, 64, 8192], P('section', None, 'tensor')
All inputs are finite; a program needn't handle non-finite values.
Results may differ from a plain program's by a relative error of at most 0.03.
Values may be sent and summed in bfloat16 or wider, within the bound.
A program may use at most 64 MiB of HBM per device.

v0:
```python
import jax
import jax.numpy as jnp
from jax import lax
from jax.sharding import PartitionSpec as P

D = 8192
HQ = 4096
RANK = 64
POWER = 2
precise = lax.Precision.HIGHEST


def from_behind(value, axis, steps):
    count = lax.axis_size(axis)
    pairs = [(source, (source + steps) % count) for source in range(count)]
    return lax.ppermute(value, axis, pairs)


def gram_of(row_block):
    return jnp.dot(row_block, row_block.T, precision=precise, preferred_element_type=jnp.float32)


def solve_rows(gram_rows, row_block):
    low_factor = jnp.linalg.cholesky(gram_rows)
    solved = lax.linalg.triangular_solve(low_factor, row_block, left_side=True, lower=True)
    return solved.astype(jnp.bfloat16)


def tokens_of(sketches, matrices):
    first_part = jnp.einsum(
        "km,tm->kt", sketches[0], matrices[0], preferred_element_type=jnp.float32
    )
    second_part = jnp.einsum(
        "km,tm->kt", sketches[1], matrices[1], preferred_element_type=jnp.float32
    )
    total_a, total_b = (
        lax.psum(first_part.astype(jnp.bfloat16), "tensor").astype(jnp.float32),
        lax.psum(second_part.astype(jnp.bfloat16), "tensor").astype(jnp.float32),
    )
    return (total_a.astype(jnp.bfloat16), total_b.astype(jnp.bfloat16))


def partials(token_rows, matrices):
    part_a = jnp.dot(token_rows[0], matrices[0], preferred_element_type=jnp.float32)
    part_b = jnp.dot(token_rows[1], matrices[1], preferred_element_type=jnp.float32)
    return (part_a, part_b)


def orthonormal(partial_value):
    part_a, part_b = partial_value
    rows_a, rows_b = (
        lax.psum(part_a.astype(jnp.bfloat16), "dp").astype(jnp.float32),
        lax.psum(part_b.astype(jnp.bfloat16), "dp").astype(jnp.float32),
    )
    gram_a, gram_b = (
        lax.psum(gram_of(rows_a).astype(jnp.bfloat16), "tensor").astype(jnp.float32),
        lax.psum(gram_of(rows_b).astype(jnp.bfloat16), "tensor").astype(jnp.float32),
    )
    basis_a = solve_rows(gram_a, rows_a)
    basis_b = solve_rows(gram_b, rows_b)
    return (basis_a, basis_b)


def body(norm_in, query_grad, attn_out, handed, sketch_q, sketch_o):
    upstream = from_behind(handed, "section", -1)
    lefts = (norm_in[0], attn_out[0])
    rights = (query_grad[0], upstream[0])
    basis = orthonormal(partials(tokens_of((sketch_q[0], sketch_o[0]), rights), lefts))
    for iteration in range(POWER):
        other = orthonormal(partials(tokens_of(basis, lefts), rights))
        basis = orthonormal(partials(tokens_of(other, rights), lefts))
    final = partials(tokens_of(basis, lefts), rights)
    raw_a, raw_b = (
        lax.psum(final[0].astype(jnp.bfloat16), "dp").astype(jnp.float32),
        lax.psum(final[1].astype(jnp.bfloat16), "dp").astype(jnp.float32),
    )
    energy_a, energy_b = lax.psum((jnp.sum(raw_a * raw_a), jnp.sum(raw_b * raw_b)), "tensor")
    adapter_aq = raw_a / jnp.sqrt(energy_a / (RANK * HQ) + 1e-06)
    adapter_ao = raw_b / jnp.sqrt(energy_b / (RANK * D) + 1e-06)
    adapter_bq = basis[0] * 16.0
    adapter_bo = basis[1] * 16.0
    return (adapter_bq[None], adapter_aq[None], adapter_bo[None], adapter_ao[None])


def solution(mesh):
    return jax.shard_map(
        body,
        mesh=mesh,
        in_specs=(
            P("section", "dp", "tensor"),
            P("section", "dp", "tensor"),
            P("section", "dp", "tensor"),
            P("section", "dp", "tensor"),
            P("section", None, "tensor"),
            P("section", None, "tensor"),
        ),
        out_specs=(
            P("section", None, "tensor"),
            P("section", None, "tensor"),
            P("section", None, "tensor"),
            P("section", None, "tensor"),
        ),
        check_vma=False,
    )
```

profile of v0, /device:TPU:32, one launch (start us, length us, event | category | flops | bytes accessed | tf_op | source)
XLA Modules:
  0.0 1890.0 jit_solution(17088234802325009747)
XLA Ops:
  7.2 7.5 collective-permute-start
  16.0 7.3 collective-permute-done
  23.6 17.3 all-reduce.17
  42.9 262.2 %all-reduce.35.cloned.1.call-done = (bf16[64,2048]{1,0:T(8,128)(2,1)}, bf16[64,1024]{1,0:T(8,128)(2,1)}) async-done(((bf16[64,2048]{1,0:T(8,128)(2,1)}, bf16[64,1024]{1,0:T(8,128)(2,1)}), (bf16[64,2048]{1,0:T(8,128)(2,1)}, bf16[64,1024]{1,0:T(8,128)(2,1)})) %all-reduce.35.cloned.1.call-update) | async-done | bytes 393232 | tf_op jit(solution)/shard_map/psum | solution.py:52
  306.5 17.1 all-reduce.16
  349.6 14.5 all-reduce.15
  366.0 251.3 %all-reduce.33.cloned.1.call-done = (bf16[64,1024]{1,0:T(8,128)(2,1)}, bf16[64,2048]{1,0:T(8,128)(2,1)}) async-done(((bf16[64,1024]{1,0:T(8,128)(2,1)}, bf16[64,2048]{1,0:T(8,128)(2,1)}), (bf16[64,1024]{1,0:T(8,128)(2,1)}, bf16[64,2048]{1,0:T(8,128)(2,1)})) %all-reduce.33.cloned.1.call-update) | async-done | bytes 393232 | tf_op jit(solution)/shard_map/psum | solution.py:52
  618.7 17.1 all-reduce.14
  635.8 5.8 cholesky.230
  648.7 5.8 cholesky.175
  661.7 14.5 all-reduce.13
  678.1 251.2 %all-reduce.31.cloned.1.call-done = (bf16[64,2048]{1,0:T(8,128)(2,1)}, bf16[64,1024]{1,0:T(8,128)(2,1)}) async-done(((bf16[64,2048]{1,0:T(8,128)(2,1)}, bf16[64,1024]{1,0:T(8,128)(2,1)}), (bf16[64,2048]{1,0:T(8,128)(2,1)}, bf16[64,1024]{1,0:T(8,128)(2,1)})) %all-reduce.31.cloned.1.call-update) | async-done | bytes 393232 | tf_op jit(solution)/shard_map/psum | solution.py:52
  930.7 17.3 all-reduce.12
  948.1 5.8 cholesky.241
  961.0 5.8 cholesky.186
  974.0 14.5 all-reduce.11
  990.3 251.2 %all-reduce.29.cloned.1.call-done = (bf16[64,1024]{1,0:T(8,128)(2,1)}, bf16[64,2048]{1,0:T(8,128)(2,1)}) async-done(((bf16[64,1024]{1,0:T(8,128)(2,1)}, bf16[64,2048]{1,0:T(8,128)(2,1)}), (bf16[64,1024]{1,0:T(8,128)(2,1)}, bf16[64,2048]{1,0:T(8,128)(2,1)})) %all-reduce.29.cloned.1.call-update) | async-done | bytes 393232 | tf_op jit(solution)/shard_map/psum | solution.py:52
  1243.0 17.1 all-reduce.10
  1286.1 14.5 all-reduce.9
  1302.5 251.1 %all-reduce.27.cloned.1.call-done = (bf16[64,2048]{1,0:T(8,128)(2,1)}, bf16[64,1024]{1,0:T(8,128)(2,1)}) async-done(((bf16[64,2048]{1,0:T(8,128)(2,1)}, bf16[64,1024]{1,0:T(8,128)(2,1)}), (bf16[64,2048]{1,0:T(8,128)(2,1)}, bf16[64,1024]{1,0:T(8,128)(2,1)})) %all-reduce.27.cloned.1.call-update) | async-done | bytes 393232 | tf_op jit(solution)/shard_map/psum | solution.py:52
  1555.0 17.3 all-reduce.8
  1598.3 14.5 all-reduce.7
  1615.3 250.7 %all-reduce.25.cloned.1.call-done = (bf16[64,1024]{1,0:T(8,128)(2,1)}, bf16[64,2048]{1,0:T(8,128)(2,1)}) async-done(((bf16[64,1024]{1,0:T(8,128)(2,1)}, bf16[64,2048]{1,0:T(8,128)(2,1)}), (bf16[64,1024]{1,0:T(8,128)(2,1)}, bf16[64,2048]{1,0:T(8,128)(2,1)})) %all-reduce.25.cloned.1.call-update) | async-done | bytes 393232 | tf_op jit(solution)/shard_map/psum | solution.py:74
  1869.1 11.1 all-reduce
  (159 shorter events, 130.9 us)
Async XLA Ops:
  7.2 33.8 %copy-start = (bf16[1,128,2048]{2,1,0:T(8,128)(2,1)S(1)}, bf16[1,128,2048]{2,1,0:T(8,128)(2,1)}, u32[]{:S(2)}) copy-start(bf16[1,128,2048]{2,1,0:T(8,128)(2,1)} %param.11) | copy-start | bytes 1572868
  7.2 16.1 copy-start.15
  7.2 297.9 %all-reduce.35.cloned.1.call-start = ((), (), s32[]{:S(2)}) async-start(), calls=%async_computation.5 | async-start | bytes 786432 | tf_op jit(solution)/shard_map/psum | solution.py:52
  7.2 16.1 collective-permute-start
  41.0 1.0 copy-start.1
  42.8 574.4 %all-reduce.33.cloned.1.call-start = ((), (), s32[]{:S(2)}) async-start(), calls=%async_computation.4 | async-start | bytes 786432 | tf_op jit(solution)/shard_map/psum | solution.py:52
  305.1 1.2 copy-start.3
  323.8 12.1 copy-start.10
  349.3 14.8 copy-start.2
  365.9 563.4 %all-reduce.31.cloned.1.call-start = ((), (), s32[]{:S(2)}) async-start(), calls=%async_computation.3 | async-start | bytes 786432 | tf_op jit(solution)/shard_map/psum | solution.py:52
  617.2 1.2 copy-start.6
  648.6 12.2 copy-start.8
  678.1 563.5 %all-reduce.29.cloned.1.call-start = ((), (), s32[]{:S(2)}) async-start(), calls=%async_computation.2 | async-start | bytes 786432 | tf_op jit(solution)/shard_map/psum | solution.py:52
  929.3 1.2 copy-start.4
  930.7 29.5 %copy-start.11 = (bf16[64,1024]{1,0:T(8,128)(2,1)S(1)}, bf16[64,1024]{1,0:T(8,128)(2,1)}, u32[]{:S(2)}) copy-start(bf16[64,1024]{1,0:T(8,128)(2,1)} %get-tuple-element.16) | copy-start | bytes 393220
  990.3 563.3 %all-reduce.27.cloned.1.call-start = ((), (), s32[]{:S(2)}) async-start(), calls=%async_computation.1 | async-start | bytes 786432 | tf_op jit(solution)/shard_map/psum | solution.py:52
  1241.6 1.2 copy-start.7
  1272.9 12.2 copy-start.9
  1302.4 563.6 %all-reduce.25.cloned.1.call-start = ((), (), s32[]{:S(2)}) async-start(), calls=%async_computation | async-start | bytes 786432 | tf_op jit(solution)/shard_map/psum | solution.py:74
  1553.6 1.2 copy-start.5
  1555.0 29.5 %copy-start.12 = (bf16[64,1024]{1,0:T(8,128)(2,1)S(1)}, bf16[64,1024]{1,0:T(8,128)(2,1)}, u32[]{:S(2)}) copy-start(bf16[64,1024]{1,0:T(8,128)(2,1)} %get-tuple-element.12) | copy-start | bytes 393220
  1866.0 1.7 copy-start.14
  1867.7 13.1 copy-start.13
Sparse Core Ops, SparseCore 0:
  42.9 262.0 all-reduce.34
  366.0 251.1 all-reduce.32
  678.2 251.0 all-reduce.30
  990.4 251.1 all-reduce.28
  1302.5 251.0 all-reduce.26
  1614.7 251.2 all-reduce.24
where the time goes:
time: 1890 us
  waiting for transfers between devices  1530 us (81%)
  blocking collectives  187 us (10%)
  other arithmetic  126 us (7%)
  matrix products  26.9 us (1%)
    psum x5, waiting for transfers between devices, orthonormal(): lax.psum(part_a.astype(jnp.bfloat16), 'dp').astype(jnp.float32)  1270 us
    psum x1, waiting for transfers between devices, body(): lax.psum(final[0].astype(jnp.bfloat16), 'dp').astype(jnp.float32)  251 us
    psum x6, blocking collectives, tokens_of(): lax.psum(first_part.astype(jnp.bfloat16), 'tensor').astype(jnp.float32)  89.9 us
    psum x5, blocking collectives, orthonormal(): lax.psum(gram_of(rows_a).astype(jnp.bfloat16), 'tensor').astype(jnp.float32)  85.8 us
    another operation x30, other arithmetic, solve_rows(): low_factor = jnp.linalg.cholesky(gram_rows)  65.2 us
    another operation x20, other arithmetic, solve_rows(): lax.linalg.triangular_solve(low_factor, row_block, left_side=True, lower=...  55.5 us
  transfers between devices with their start and end apart: 7, of which 7 were waited for; matrix products, arithmetic and copies ran while one was open for 0% of the time, Pallas kernels for 0%

commit v1 on v0

--- a/solution.py
+++ b/solution.py
@@ -71,7 +71,9 @@
         basis = orthonormal(partials(tokens_of(other, rights), lefts))
     final = partials(tokens_of(basis, lefts), rights)
     raw_a, raw_b = (
-        lax.psum(final[0].astype(jnp.bfloat16), "dp").astype(jnp.float32),
+        jnp.sum(lax.all_gather(final[0].astype(jnp.bfloat16), axis_name="dp"), 0).astype(
+            jnp.float32
+        ),
         lax.psum(final[1].astype(jnp.bfloat16), "dp").astype(jnp.float32),
     )
     energy_a, energy_b = lax.psum((jnp.sum(raw_a * raw_a), jnp.sum(raw_b * raw_b)), "tensor")

time: 1890 us -> 2020 us (1.069)
  the two profiles are of different devices: /device:TPU:32 before, /device:TPU:2 now
where the time goes in v1:
time: 2020 us
  waiting for transfers between devices  1610 us (80%)
  blocking collectives  217 us (11%)
  other arithmetic  127 us (6%)
  matrix products  41.3 us (2%)
    psum x5, waiting for transfers between devices, orthonormal(): lax.psum(part_a.astype(jnp.bfloat16), 'dp').astype(jnp.float32)  1260 us
    psum x1, waiting for transfers between devices, orthonormal(): lax.psum(part_b.astype(jnp.bfloat16), 'dp').astype(jnp.float32)  242 us
    all_gather x1, waiting for transfers between devices, body(): lax.all_gather(final[0].astype(jnp.bfloat16), axis_name='dp')  93.5 us
    psum x6, blocking collectives, tokens_of(): lax.psum(first_part.astype(jnp.bfloat16), 'tensor').astype(jnp.float32)  86.6 us
    psum x5, blocking collectives, orthonormal(): lax.psum(gram_of(rows_a).astype(jnp.bfloat16), 'tensor').astype(jnp.float32)  85.3 us
    another operation x30, other arithmetic, solve_rows(): low_factor = jnp.linalg.cholesky(gram_rows)  65.2 us
    another operation x20, other arithmetic, solve_rows(): lax.linalg.triangular_solve(low_factor, row_block, left_side=True, lower=...  55.5 us
  transfers between devices with their start and end apart: 8, of which 8 were waited for; matrix products, arithmetic and copies ran while one was open for 0% of the time, Pallas kernels for 0%

profile of v1, /device:TPU:2, one launch (start us, length us, event | category | flops | bytes accessed | tf_op | source)
XLA Modules:
  0.0 2023.7 jit_solution(875634426033747834)
XLA Ops:
  7.2 13.3 collective-permute-start
  20.5 11.5 collective-permute-done
  33.3 17.2 psum.262
  53.5 242.3 %all-reduce.22.cloned.1.call-done = bf16[64,1024]{1,0:T(8,128)(2,1)} async-done(((bf16[64,1024]{1,0:T(8,128)(2,1)}), bf16[64,1024]{1,0:T(8,128)(2,1)}) %all-reduce.22.cloned.1.call-update) | async-done | bytes 131088 | tf_op jit(solution)/shard_map/psum | solution.py:53
  297.0 16.9 psum.264
  327.7 14.5 all-reduce.14
  344.1 252.9 %all-reduce.32.cloned.1.call-done = (bf16[64,2048]{1,0:T(8,128)(2,1)}, bf16[64,2048]{1,0:T(8,128)(2,1)}) async-done(((bf16[64,2048]{1,0:T(8,128)(2,1)}, bf16[64,2048]{1,0:T(8,128)(2,1)}), (bf16[64,2048]{1,0:T(8,128)(2,1)}, bf16[64,2048]{1,0:T(8,128)(2,1)})) %all-reduce.32.cloned.1.call-update) | async-done | bytes 524304 | tf_op jit(solution)/shard_map/psum | solution.py:52
  599.6 17.1 all-reduce.13
  643.9 14.5 all-reduce.12
  660.1 250.6 %all-reduce.30.cloned.1.call-done = (bf16[64,1024]{1,0:T(8,128)(2,1)}, bf16[64,1024]{1,0:T(8,128)(2,1)}) async-done(((bf16[64,1024]{1,0:T(8,128)(2,1)}, bf16[64,1024]{1,0:T(8,128)(2,1)}), (bf16[64,1024]{1,0:T(8,128)(2,1)}, bf16[64,1024]{1,0:T(8,128)(2,1)})) %all-reduce.30.cloned.1.call-update) | async-done | bytes 262160 | tf_op jit(solution)/shard_map/psum | solution.py:52
  913.1 17.1 all-reduce.11
  944.0 5.8 cholesky.175
  957.6 14.5 all-reduce.10
  974.0 253.1 %all-reduce.28.cloned.1.call-done = (bf16[64,2048]{1,0:T(8,128)(2,1)}, bf16[64,2048]{1,0:T(8,128)(2,1)}) async-done(((bf16[64,2048]{1,0:T(8,128)(2,1)}, bf16[64,2048]{1,0:T(8,128)(2,1)}), (bf16[64,2048]{1,0:T(8,128)(2,1)}, bf16[64,2048]{1,0:T(8,128)(2,1)})) %all-reduce.28.cloned.1.call-update) | async-done | bytes 524304 | tf_op jit(solution)/shard_map/psum | solution.py:52
  1229.7 17.1 all-reduce.9
  1274.0 14.5 all-reduce.8
  1290.2 250.6 %all-reduce.26.cloned.1.call-done = (bf16[64,1024]{1,0:T(8,128)(2,1)}, bf16[64,1024]{1,0:T(8,128)(2,1)}) async-done(((bf16[64,1024]{1,0:T(8,128)(2,1)}, bf16[64,1024]{1,0:T(8,128)(2,1)}), (bf16[64,1024]{1,0:T(8,128)(2,1)}, bf16[64,1024]{1,0:T(8,128)(2,1)})) %all-reduce.26.cloned.1.call-update) | async-done | bytes 262160 | tf_op jit(solution)/shard_map/psum | solution.py:52
  1543.2 17.1 all-reduce.7
  1587.7 14.5 all-reduce.6
  1604.1 253.0 %all-reduce.24.cloned.1.call-done = (bf16[64,2048]{1,0:T(8,128)(2,1)}, bf16[64,2048]{1,0:T(8,128)(2,1)}) async-done(((bf16[64,2048]{1,0:T(8,128)(2,1)}, bf16[64,2048]{1,0:T(8,128)(2,1)}), (bf16[64,2048]{1,0:T(8,128)(2,1)}, bf16[64,2048]{1,0:T(8,128)(2,1)})) %all-reduce.24.cloned.1.call-update) | async-done | bytes 524304 | tf_op jit(solution)/shard_map/psum | solution.py:52
  1858.4 16.9 psum.259
  1889.4 14.3 psum.260
  1906.0 93.5 %all-gather.3.cloned.1.call-done = bf16[1024,1024]{1,0:T(8,128)(2,1)} async-done(((bf16[64,1024]{1,0:T(8,128)(2,1)}), bf16[1024,1024]{1,0:T(8,128)(2,1)}) %all-gather.3.cloned.1.call-update) | async-done | bytes 2097168 | tf_op jit(solution)/shard_map/all_gather | solution.py:74
  2002.8 11.1 all-reduce
  (145 shorter events, 163.9 us)
Async XLA Ops:
  7.2 335.0 %copy-start = (bf16[1,128,2048]{2,1,0:T(8,128)(2,1)S(1)}, bf16[1,128,2048]{2,1,0:T(8,128)(2,1)}, u32[]{:S(2)}) copy-start(bf16[1,128,2048]{2,1,0:T(8,128)(2,1)} %param.11) | copy-start | bytes 1572868
  7.2 320.3 %copy-start.1 = (bf16[1,128,1024]{2,1,0:T(8,128)(2,1)S(1)}, bf16[1,128,1024]{2,1,0:T(8,128)(2,1)}, u32[]{:S(2)}) copy-start(bf16[1,128,1024]{2,1,0:T(8,128)(2,1)} %param.13) | copy-start | bytes 786436
  7.2 288.7 %all-reduce.22.cloned.1.call-start = ((), (), s32[]{:S(2)}) async-start(), calls=%async_computation | async-start | bytes 262144 | tf_op jit(solution)/shard_map/psum | solution.py:53
  7.2 24.8 %collective-permute-start = (bf16[1,128,2048]{2,1,0:T(8,128)(2,1)}, bf16[1,128,2048]{2,1,0:T(8,128)(2,1)S(1)}, u32[]{:S(2)}, u32[]{:S(2)}) collective-permute-start(bf16[1,128,2048]{2,1,0:T(8,128)(2,1)} %param.14), channel_id=1, source_target_pairs={{0,448},{64,0},{128,64},{192,128},{256,192},{320,256},{384,320},{4... | collective-permute-start | bytes 1572872 | tf_op jit(solution)/shard_map/ppermute | solution.py:16
  52.2 544.8 %all-reduce.32.cloned.1.call-start = ((), (), s32[]{:S(2)}) async-start(), calls=%async_computation.6 | async-start | bytes 1048576 | tf_op jit(solution)/shard_map/psum | solution.py:52
  344.0 566.8 %all-reduce.30.cloned.1.call-start = ((), (), s32[]{:S(2)}) async-start(), calls=%async_computation.5 | async-start | bytes 524288 | tf_op jit(solution)/shard_map/psum | solution.py:52
  597.0 45.7 %copy-start.3 = (bf16[64,2048]{1,0:T(8,128)(2,1)S(1)}, bf16[64,2048]{1,0:T(8,128)(2,1)}, u32[]{:S(2)}) copy-start(bf16[64,2048]{1,0:T(8,128)(2,1)} %get-tuple-element.17) | copy-start | bytes 786436
  598.3 60.9 %copy-start.2 = (bf16[1,128,1024]{2,1,0:T(8,128)(2,1)S(1)}, bf16[1,128,1024]{2,1,0:T(8,128)(2,1)}, u32[]{:S(2)}) copy-start(bf16[1,128,1024]{2,1,0:T(8,128)(2,1)} %param.12) | copy-start | bytes 786436
  660.1 567.1 %all-reduce.28.cloned.1.call-start = ((), (), s32[]{:S(2)}) async-start(), calls=%async_computation.4 | async-start | bytes 1048576 | tf_op jit(solution)/shard_map/psum | solution.py:52
  974.0 566.9 %all-reduce.26.cloned.1.call-start = ((), (), s32[]{:S(2)}) async-start(), calls=%async_computation.3 | async-start | bytes 524288 | tf_op jit(solution)/shard_map/psum | solution.py:52
  1227.1 45.6 %copy-start.4 = (bf16[64,2048]{1,0:T(8,128)(2,1)S(1)}, bf16[64,2048]{1,0:T(8,128)(2,1)}, u32[]{:S(2)}) copy-start(bf16[64,2048]{1,0:T(8,128)(2,1)} %get-tuple-element.13) | copy-start | bytes 786436
  1290.2 567.0 %all-reduce.24.cloned.1.call-start = ((), (), s32[]{:S(2)}) async-start(), calls=%async_computation.2 | async-start | bytes 1048576 | tf_op jit(solution)/shard_map/psum | solution.py:52
  1604.1 395.4 %all-gather.3.cloned.1.call-start = ((), (), s32[]{:S(2)}) async-start(), calls=%async_computation.1 | async-start | bytes 2228224 | tf_op jit(solution)/shard_map/all_gather | solution.py:74
  1857.1 48.1 %copy-start.5 = (bf16[64,2048]{1,0:T(8,128)(2,1)S(1)}, bf16[64,2048]{1,0:T(8,128)(2,1)}, u32[]{:S(2)}) copy-start(bf16[64,2048]{1,0:T(8,128)(2,1)} %get-tuple-element.10) | copy-start | bytes 786436
Sparse Core Ops, SparseCore 0:
  52.4 243.4 all-reduce.21
  344.1 252.8 all-reduce.31
  660.2 250.5 all-reduce.29
  974.1 252.9 all-reduce.27
  1290.3 250.5 all-reduce.25
  1604.2 252.8 all-reduce.23
  1904.7 94.7 all-gather.2
